TPU v7x, 32 devices: a whole 2x2x4 slice. The times are simulated.
32 devices in a mesh: gx: 4 (over y, x), gy: 2 (over core), gz: 4 (over z).
Axes of the slice: x: 2, y: 2, z: 4, core: 2. Of those that a mesh axis runs over, the one named last changes fastest.
Arguments:
- tokens: bfloat16 [192, 12288], P(('gy', 'gz'), 'gx'), may hold values from -6 to 6
- grad_out: bfloat16 [192, 12288], P(('gy', 'gz'), 'gx'), may hold values from -0.86328125 to 0.86328125
- w_in: bfloat16 [12288, 24576], P('gx', ('gy', 'gz')), may hold values from -0.0546875 to 0.0546875
- w_out: bfloat16 [24576, 12288], P(('gy', 'gz'), 'gx'), may hold values from -0.0390625 to 0.0390625
Outputs:
- output: float32 [192, 12288], P(('gy', 'gz'), 'gx')
- grad_in: float32 [192, 12288], P(('gy', 'gz'), 'gx')
- grad_w_in: bfloat16 [12288, 24576], P('gx', ('gy', 'gz'))
- grad_w_out: bfloat16 [24576, 12288], P(('gy', 'gz'), 'gx')
All inputs are finite; a program needn't handle non-finite values.
Results may differ from a plain program's by a relative error of at most 0.0049.
Values may be sent and summed in bfloat16 or wider, within the bound.
A program may use at most 128 MiB of HBM per device.

v0:
```python
import jax
import jax.numpy as jnp
from jax import lax
from jax.sharding import PartitionSpec as P


def activate(pre_sum, back_sum):
    scale_c = 0.7978845608
    inner_arg = scale_c * (pre_sum + 0.044715 * pre_sum * pre_sum * pre_sum)
    tanh_val = jnp.tanh(inner_arg)
    value = 0.5 * pre_sum * (1.0 + tanh_val)
    deriv = 0.5 * (1.0 + tanh_val) + 0.5 * pre_sum * (1.0 - tanh_val * tanh_val) * scale_c * (
        1.0 + 3.0 * 0.044715 * pre_sum * pre_sum
    )
    return (value.astype(jnp.bfloat16), (back_sum * deriv).astype(jnp.bfloat16))


def right_product(left, right):
    return lax.dot_general(
        left, right, (((1,), (1,)), ((), ())), preferred_element_type=jnp.float32
    )


def left_product(left, right):
    return lax.dot_general(
        left, right, (((0,), (0,)), ((), ())), preferred_element_type=jnp.float32
    )


def shards(tokens, grad_out, w_in, w_out):
    token_rows, grad_rows = (
        lax.all_gather(tokens, ("gy", "gz"), axis=0, tiled=True),
        lax.all_gather(grad_out, ("gy", "gz"), axis=0, tiled=True),
    )
    pre_part = jnp.dot(token_rows, w_in, preferred_element_type=jnp.float32)
    back_part = right_product(grad_rows, w_out)
    pre_sum, back_sum = lax.psum((pre_part, back_part), "gx")
    hidden, slopes = activate(pre_sum, back_sum)
    picked = hidden
    output = lax.psum_scatter(
        jnp.dot(picked, w_out, preferred_element_type=jnp.float32),
        ("gy", "gz"),
        scatter_dimension=0,
        tiled=True,
    )
    picked = slopes
    grad_in = lax.psum_scatter(
        right_product(picked, w_in), ("gy", "gz"), scatter_dimension=0, tiled=True
    )
    grad_w_in = left_product(token_rows, slopes).astype(jnp.bfloat16)
    grad_w_out = left_product(hidden, grad_rows).astype(jnp.bfloat16)
    return (output, grad_in, grad_w_in, grad_w_out)


def solution(mesh):
    placed = (
        P(("gy", "gz"), "gx"),
        P(("gy", "gz"), "gx"),
        P("gx", ("gy", "gz")),
        P(("gy", "gz"), "gx"),
    )
    return jax.shard_map(
        shards,
        mesh=mesh,
        in_specs=placed,
        out_specs=(
            P(("gy", "gz"), "gx"),
            P(("gy", "gz"), "gx"),
            P("gx", ("gy", "gz")),
            P(("gy", "gz"), "gx"),
        ),
        check_vma=False,
    )
```

profile of v0, /device:TPU:0, one launch (start us, length us, event | category | flops | bytes accessed | tf_op | source)
XLA Modules:
  0.0 315.6 jit_solution(16967540374349955192)
XLA Ops:
  7.2 0.0 all-gather.3.cloned.1.call-start
  7.2 0.7 all-gather.3.cloned.1.call-update
  7.9 0.0 all-gather.5.cloned.1.call-start
  7.9 0.7 all-gather.5.cloned.1.call-update
  8.6 0.0 all-reduce.3.cloned.1.call-start
  8.7 26.3 %all-gather.3.cloned.1.call-done = bf16[192,3072]{1,0:T(8,128)(2,1)} async-done(((bf16[24,3072]{1,0:T(8,128)(2,1)}), bf16[192,3072]{1,0:T(8,128)(2,1)}) %all-gather.3.cloned.1.call-update) | async-done | bytes 1179664 | tf_op jit(solution)/shard_map/all_gather | solution.py:32
  35.0 12.0 %fusion.8 = f32[192,3072]{1,0:T(8,128)} fusion(bf16[192,3072]{1,0:T(8,128)(2,1)} %all-gather.3.cloned.1.call-done, bf16[3072,3072]{1,0:T(8,128)(2,1)} %param.6), kind=kOutput, calls=%fused_computation.13 | convolution fusion | flops 3623878656 | bytes 22413312 | tf_op jit(solution)/shard_map/dot_general | solution.py:35
  47.0 12.1 %all-gather.5.cloned.1.call-done = bf16[192,3072]{1,0:T(8,128)(2,1)} async-done(((bf16[24,3072]{1,0:T(8,128)(2,1)}), bf16[192,3072]{1,0:T(8,128)(2,1)}) %all-gather.5.cloned.1.call-update) | async-done | bytes 1179664 | tf_op jit(solution)/shard_map/all_gather | solution.py:33
  59.0 14.5 %fusion.9 = f32[192,3072]{1,0:T(8,128)} fusion(bf16[192,3072]{1,0:T(8,128)(2,1)} %all-gather.5.cloned.1.call-done, bf16[3072,3072]{1,0:T(8,128)(2,1)} %param.7), kind=kOutput, calls=%fused_computation.14 | convolution fusion | flops 3623878656 | bytes 22413312 | tf_op jit(solution)/shard_map/dot_general | solution.py:19
  73.5 0.0 all-reduce.3.cloned.1.call-update
  73.6 0.0 reduce-scatter.3.cloned.1.call-start
  73.6 112.7 %all-reduce.3.cloned.1.call-done = (f32[192,3072]{1,0:T(8,128)}, f32[192,3072]{1,0:T(8,128)}) async-done(((f32[192,3072]{1,0:T(8,128)}, f32[192,3072]{1,0:T(8,128)}), (f32[192,3072]{1,0:T(8,128)}, f32[192,3072]{1,0:T(8,128)})) %all-reduce.3.cloned.1.call-update) | async-done | bytes 4718608 | tf_op jit(solution)/shard_map/psum | solution.py:37
  186.3 12.6 %fusion.7 = f32[192,3072]{1,0:T(8,128)} fusion(bf16[3072,3072]{1,0:T(8,128)(2,1)} %param.7, f32[192,3072]{1,0:T(8,128)} %get-tuple-element.8), kind=kOutput, calls=%fused_computation.12 | convolution fusion | flops 3629187072 | bytes 23592960 | tf_op jit(solution)/shard_map/dot_general | solution.py:41
  198.9 0.0 copy-start
  198.9 0.0 reduce-scatter.3.cloned.1.call-update
  198.9 0.2 reduce-scatter.5.cloned.1.call-start
  199.2 1.4 copy-done
  200.6 3.1 fusion.6
  203.7 11.7 %fusion.10 = f32[192,3072]{1,0:T(8,128)} fusion(bf16[192,3072]{1,0:T(8,128)(2,1)S(1)} %fusion.6, bf16[3072,3072]{1,0:T(8,128)(2,1)} %param.6), kind=kOutput, calls=%fused_computation.15 | convolution fusion | flops 3623878656 | bytes 22413312 | tf_op jit(solution)/shard_map/dot_general | solution.py:19
  215.5 0.0 reduce-scatter.5.cloned.1.call-update
  215.5 10.8 %convert_bitcast_fusion = bf16[3072,3072]{0,1:T(8,128)(2,1)} fusion(bf16[192,3072]{1,0:T(8,128)(2,1)S(1)} %fusion.6, bf16[192,3072]{1,0:T(8,128)(2,1)} %all-gather.3.cloned.1.call-done), kind=kOutput, calls=%fused_computation | convolution fusion | flops 3633315840 | bytes 21233664 | tf_op jit(solution)/shard_map/dot_general | solution.py:25
  226.3 0.0 copy-start.1
  226.3 24.7 %copy.8 = bf16[3072,3072]{1,0:T(8,128)(2,1)} copy(bf16[3072,3072]{0,1:T(8,128)(2,1)} %convert_bitcast_fusion) | data formatting | bytes 37748736
  251.0 0.0 copy-done.1
  251.0 9.6 %convolution_convert_fusion = bf16[3072,3072]{1,0:T(8,128)(2,1)} fusion(bf16[192,3072]{1,0:T(8,128)(2,1)S(1)} %copy-done.1, f32[192,3072]{1,0:T(8,128)S(1)} %copy-done), kind=kOutput, calls=%fused_computation.1 | convolution fusion | flops 3638624256 | bytes 22413312 | tf_op jit(solution)/shard_map/dot_general | solution.py:25
  260.6 0.0 reduce-scatter.3.cloned.1.call-done
  260.6 48.5 %reduce-scatter.5.cloned.1.call-done = f32[24,3072]{1,0:T(8,128)} async-done(((f32[192,3072]{1,0:T(8,128)}), f32[24,3072]{1,0:T(8,128)}) %reduce-scatter.5.cloned.1.call-update) | async-done | bytes 294928 | tf_op jit(solution)/shard_map/reduce_scatter | solution.py:47
Async XLA Ops:
  7.2 27.8 %all-gather.3.cloned.1.call-start = ((), (), s32[]{:S(2)}) async-start(), calls=%async_computation.2 | async-start | bytes 1327104 | tf_op jit(solution)/shard_map/all_gather | solution.py:32
  7.9 51.1 %all-gather.5.cloned.1.call-start = ((), (), s32[]{:S(2)}) async-start(), calls=%async_computation.4 | async-start | bytes 1327104 | tf_op jit(solution)/shard_map/all_gather | solution.py:33
  8.6 177.7 %all-reduce.3.cloned.1.call-start = ((), (), s32[]{:S(2)}) async-start(), calls=%async_computation.6 | async-start | bytes 9437184 | tf_op jit(solution)/shard_map/psum | solution.py:37
  73.6 187.0 %reduce-scatter.3.cloned.1.call-start = ((), (), s32[]{:S(2)}) async-start(), calls=%async_computation.3 | async-start | bytes 2654208 | tf_op jit(solution)/shard_map/reduce_scatter | solution.py:40
  198.9 1.7 copy-start
  198.9 110.1 %reduce-scatter.5.cloned.1.call-start = ((), (), s32[]{:S(2)}) async-start(), calls=%async_computation.5 | async-start | bytes 2654208 | tf_op jit(solution)/shard_map/reduce_scatter | solution.py:47
  226.3 24.7 %copy-start.1 = (bf16[192,3072]{1,0:T(8,128)(2,1)S(1)}, bf16[192,3072]{1,0:T(8,128)(2,1)}, u32[]{:S(2)}) copy-start(bf16[192,3072]{1,0:T(8,128)(2,1)} %all-gather.5.cloned.1.call-done) | copy-start | bytes 3538948
Sparse Core Ops, SparseCore 0:
  9.6 25.3 all-gather.2
  36.6 22.4 all-gather.4
  73.7 112.6 all-reduce.2
  199.1 54.0 reduce-scatter.2
  255.9 53.1 reduce-scatter.4
where the time goes:
time: 316 us
  waiting for transfers between devices  201 us (64%)
  matrix products  71.1 us (22%)
  local copies, waits for them, and re-layouts  26.1 us (8%)
  between operations  13.8 us (4%)
    psum x1, waiting for transfers between devices, shards(): pre_sum, back_sum = lax.psum((pre_part, back_part), 'gx')  113 us
    reduce_scatter x1, waiting for transfers between devices, shards(): lax.psum_scatter(right_product(picked, w_in), ('gy', 'gz'), scatter_dimen...  48.5 us
    all_gather x1, waiting for transfers between devices, shards(): lax.all_gather(tokens, ('gy', 'gz'), axis=0, tiled=True)  26.3 us
    dot_general x2, matrix products, right_product(): lax.dot_general(left, right, (((1,), (1,)), ((), ())), preferred_element_...  26.2 us
    unnamed x5, local copies, waits for them, and re-layouts  26.1 us
    dot_general x2, matrix products, left_product(): lax.dot_general(left, right, (((0,), (0,)), ((), ())), preferred_element_...  20.4 us
    dot_general x1, matrix products, shards(): jnp.dot(picked, w_out, preferred_element_type=jnp.float32)  12.6 us
    all_gather x1, waiting for transfers between devices, shards(): lax.all_gather(grad_out, ('gy', 'gz'), axis=0, tiled=True)  12.1 us
  transfers between devices with their start and end apart: 5, of which 4 were waited for; matrix products, arithmetic and copies ran while one was open for 23% of the time, Pallas kernels for 0%

commit v1 on v0

--- a/solution.py
+++ b/solution.py
@@ -2,6 +2,17 @@
 import jax.numpy as jnp
 from jax import lax
 from jax.sharding import PartitionSpec as P
+
+
+def gather_around(x, axis, dim):
+    ways = lax.axis_size(axis)
+    pieces = [x]
+    for far in range(1, ways):
+        pieces.append(
+            lax.ppermute(pieces[far - 1], axis, [(d, (d - 1) % ways) for d in range(ways)])
+        )
+    line = jnp.concatenate(pieces, axis=dim)
+    return jnp.roll(line, lax.axis_index(axis) * x.shape[dim], axis=dim)
 
 
 def activate(pre_sum, back_sum):
@@ -29,7 +40,7 @@
 
 def shards(tokens, grad_out, w_in, w_out):
     token_rows, grad_rows = (
-        lax.all_gather(tokens, ("gy", "gz"), axis=0, tiled=True),
+        gather_around(tokens, ("gy", "gz"), 0),
         lax.all_gather(grad_out, ("gy", "gz"), axis=0, tiled=True),
     )
     pre_part = jnp.dot(token_rows, w_in, preferred_element_type=jnp.float32)

time: 316 us -> 340 us (1.076)
  starting transfers between devices: 0.38 us -> 26.7 us
  local copies, waits for them, and re-layouts: 26.1 us -> 2.55 us
  waiting for transfers between devices: 201 us -> 224 us
    reduce_scatter x1, waiting for transfers between devices: 0.01 us -> 56 us  [shards(): lax.psum_scatter(jnp.dot(picked, w_out, preferred_element_type=jnp.float3...]
    ppermute x0 -> x7, waiting for transfers between devices: none -> 32.5 us  [gather_around(): lax.ppermute(pieces[far - 1], axis, [(d, (d - 1) % ways) for d in range(w...]
    reduce_scatter x1, waiting for transfers between devices: 48.5 us -> 19.9 us  [shards(): lax.psum_scatter(right_product(picked, w_in), ('gy', 'gz'), scatter_dimen...]
    ppermute x0 -> x7, starting transfers between devices: none -> 26.4 us  [gather_around(): lax.ppermute(pieces[far - 1], axis, [(d, (d - 1) % ways) for d in range(w...]
    all_gather x1 -> x0, waiting for transfers between devices: 26.3 us -> none  [shards(): lax.all_gather(tokens, ('gy', 'gz'), axis=0, tiled=True)]
    unnamed x5 -> x23, local copies, waits for them, and re-layouts: 26.1 us -> 2.53 us
    all_gather x1, waiting for transfers between devices: 12.1 us -> 0.01 us  [shards(): lax.all_gather(grad_out, ('gy', 'gz'), axis=0, tiled=True)]
  transfers between devices with their start and end apart: 5 -> 11, of which waited for: 4 -> 10; matrix products, arithmetic and copies ran while one was open for 23% -> 13% of each run, Pallas kernels for 0% -> 0%
where the time goes in v1:
time: 340 us
  waiting for transfers between devices  224 us (66%)
  matrix products  69.3 us (20%)
  starting transfers between devices  26.7 us (8%)
  between operations  13.9 us (4%)
  other arithmetic  3.86 us (1%)
    psum x1, waiting for transfers between devices, shards(): pre_sum, back_sum = lax.psum((pre_part, back_part), 'gx')  115 us
    reduce_scatter x1, waiting for transfers between devices, shards(): lax.psum_scatter(jnp.dot(picked, w_out, preferred_element_type=jnp.float3...  56 us
    ppermute x7, waiting for transfers between devices, gather_around(): lax.ppermute(pieces[far - 1], axis, [(d, (d - 1) % ways) for d in range(w...  32.5 us
    ppermute x7, starting transfers between devices, gather_around(): lax.ppermute(pieces[far - 1], axis, [(d, (d - 1) % ways) for d in range(w...  26.4 us
    dot_general x2, matrix products, right_product(): lax.dot_general(left, right, (((1,), (1,)), ((), ())), preferred_element_...  26 us
    dot_general x2, matrix products, left_product(): lax.dot_general(left, right, (((0,), (0,)), ((), ())), preferred_element_...  20.5 us
    reduce_scatter x1, waiting for transfers between devices, shards(): lax.psum_scatter(right_product(picked, w_in), ('gy', 'gz'), scatter_dimen...  19.9 us
    dot_general x1, matrix products, shards(): jnp.dot(picked, w_out, preferred_element_type=jnp.float32)  12.1 us
  transfers between devices with their start and end apart: 11, of which 10 were waited for; matrix products, arithmetic and copies ran while one was open for 13% of the time, Pallas kernels for 0%

profile of v1, /device:TPU:0, one launch (start us, length us, event | category | flops | bytes accessed | tf_op | source)
XLA Modules:
  0.0 340.1 jit_solution(4537127508412714284)
XLA Ops:
  7.2 0.0 copy-start.3
  7.2 0.0 all-gather.2.cloned.1.call-start
  7.2 0.7 all-gather.2.cloned.1.call-update
  7.9 0.0 all-reduce.3.cloned.1.call-start
  8.0 4.5 %collective-permute-start = (bf16[24,3072]{1,0:T(8,128)(2,1)}, bf16[24,3072]{1,0:T(8,128)(2,1)S(1)}, u32[]{:S(2)}, u32[]{:S(2)}) collective-permute-start(bf16[24,3072]{1,0:T(8,128)(2,1)} %param.4), channel_id=1, source_target_pairs={{0,7},{1,0},{2,1},{3,2},{4,3},{5,4},{6,5},{7,6},{8,15},{9,8},{10,9... | collective-permute-start | bytes 442376 | tf_op jit(solution)/shard_map/ppermute | solution.py:12
  12.5 1.0 constant_dynamic-update-slice_fusion.15
  13.5 3.6 %collective-permute-done = bf16[24,3072]{1,0:T(8,128)(2,1)S(1)} collective-permute-done((bf16[24,3072]{1,0:T(8,128)(2,1)}, bf16[24,3072]{1,0:T(8,128)(2,1)S(1)}, u32[]{:S(2)}, u32[]{:S(2)}) %collective-permute-start) | collective-permute-done | bytes 147488 | tf_op jit(solution)/shard_map/ppermute | solution.py:12
  17.0 3.9 %collective-permute-start.1 = (bf16[24,3072]{1,0:T(8,128)(2,1)S(1)}, bf16[24,3072]{1,0:T(8,128)(2,1)S(1)}, u32[]{:S(2)}, u32[]{:S(2)}) collective-permute-start(bf16[24,3072]{1,0:T(8,128)(2,1)S(1)} %collective-permute-done), channel_id=1, source_target_pairs={{0,7},{1,0},{2,1},{3,2},{4,3},{5,4},{6,5},{7,6},{8,15},{9,8},{10,9... | collective-permute-start | bytes 442376 | tf_op jit(solution)/shard_map/ppermute | solution.py:12
  20.9 7.2 %collective-permute-done.1 = bf16[24,3072]{1,0:T(8,128)(2,1)S(1)} collective-permute-done((bf16[24,3072]{1,0:T(8,128)(2,1)S(1)}, bf16[24,3072]{1,0:T(8,128)(2,1)S(1)}, u32[]{:S(2)}, u32[]{:S(2)}) %collective-permute-start.1) | collective-permute-done | bytes 147488 | tf_op jit(solution)/shard_map/ppermute | solution.py:12
  28.1 3.7 %collective-permute-start.2 = (bf16[24,3072]{1,0:T(8,128)(2,1)S(1)}, bf16[24,3072]{1,0:T(8,128)(2,1)S(1)}, u32[]{:S(2)}, u32[]{:S(2)}) collective-permute-start(bf16[24,3072]{1,0:T(8,128)(2,1)S(1)} %collective-permute-done.1), channel_id=1, source_target_pairs={{0,7},{1,0},{2,1},{3,2},{4,3},{5,4},{6,5},{7,6},{8,15},{9,8},{10,9... | collective-permute-start | bytes 442376 | tf_op jit(solution)/shard_map/ppermute | solution.py:12
  31.9 6.0 %collective-permute-done.2 = bf16[24,3072]{1,0:T(8,128)(2,1)S(1)} collective-permute-done((bf16[24,3072]{1,0:T(8,128)(2,1)S(1)}, bf16[24,3072]{1,0:T(8,128)(2,1)S(1)}, u32[]{:S(2)}, u32[]{:S(2)}) %collective-permute-start.2) | collective-permute-done | bytes 147488 | tf_op jit(solution)/shard_map/ppermute | solution.py:12
  37.9 3.1 collective-permute-start.3
  41.0 3.9 %collective-permute-done.3 = bf16[24,3072]{1,0:T(8,128)(2,1)S(1)} collective-permute-done((bf16[24,3072]{1,0:T(8,128)(2,1)S(1)}, bf16[24,3072]{1,0:T(8,128)(2,1)S(1)}, u32[]{:S(2)}, u32[]{:S(2)}) %collective-permute-start.3) | collective-permute-done | bytes 147488 | tf_op jit(solution)/shard_map/ppermute | solution.py:12
  44.9 3.7 %collective-permute-start.4 = (bf16[24,3072]{1,0:T(8,128)(2,1)S(1)}, bf16[24,3072]{1,0:T(8,128)(2,1)S(1)}, u32[]{:S(2)}, u32[]{:S(2)}) collective-permute-start(bf16[24,3072]{1,0:T(8,128)(2,1)S(1)} %collective-permute-done.3), channel_id=1, source_target_pairs={{0,7},{1,0},{2,1},{3,2},{4,3},{5,4},{6,5},{7,6},{8,15},{9,8},{10,9... | collective-permute-start | bytes 442376 | tf_op jit(solution)/shard_map/ppermute | solution.py:12
  48.6 3.9 %collective-permute-done.4 = bf16[24,3072]{1,0:T(8,128)(2,1)S(1)} collective-permute-done((bf16[24,3072]{1,0:T(8,128)(2,1)S(1)}, bf16[24,3072]{1,0:T(8,128)(2,1)S(1)}, u32[]{:S(2)}, u32[]{:S(2)}) %collective-permute-start.4) | collective-permute-done | bytes 147488 | tf_op jit(solution)/shard_map/ppermute | solution.py:12
  52.6 3.7 %collective-permute-start.5 = (bf16[24,3072]{1,0:T(8,128)(2,1)S(1)}, bf16[24,3072]{1,0:T(8,128)(2,1)S(1)}, u32[]{:S(2)}, u32[]{:S(2)}) collective-permute-start(bf16[24,3072]{1,0:T(8,128)(2,1)S(1)} %collective-permute-done.4), channel_id=1, source_target_pairs={{0,7},{1,0},{2,1},{3,2},{4,3},{5,4},{6,5},{7,6},{8,15},{9,8},{10,9... | collective-permute-start | bytes 442376 | tf_op jit(solution)/shard_map/ppermute | solution.py:12
  56.3 3.9 %collective-permute-done.5 = bf16[24,3072]{1,0:T(8,128)(2,1)S(1)} collective-permute-done((bf16[24,3072]{1,0:T(8,128)(2,1)S(1)}, bf16[24,3072]{1,0:T(8,128)(2,1)S(1)}, u32[]{:S(2)}, u32[]{:S(2)}) %collective-permute-start.5) | collective-permute-done | bytes 147488 | tf_op jit(solution)/shard_map/ppermute | solution.py:12
  60.2 3.7 %collective-permute-start.6 = (bf16[24,3072]{1,0:T(8,128)(2,1)S(1)}, bf16[24,3072]{1,0:T(8,128)(2,1)S(1)}, u32[]{:S(2)}, u32[]{:S(2)}) collective-permute-start(bf16[24,3072]{1,0:T(8,128)(2,1)S(1)} %collective-permute-done.5), channel_id=1, source_target_pairs={{0,7},{1,0},{2,1},{3,2},{4,3},{5,4},{6,5},{7,6},{8,15},{9,8},{10,9... | collective-permute-start | bytes 442376 | tf_op jit(solution)/shard_map/ppermute | solution.py:12
  63.9 3.9 %collective-permute-done.6 = bf16[24,3072]{1,0:T(8,128)(2,1)S(1)} collective-permute-done((bf16[24,3072]{1,0:T(8,128)(2,1)S(1)}, bf16[24,3072]{1,0:T(8,128)(2,1)S(1)}, u32[]{:S(2)}, u32[]{:S(2)}) %collective-permute-start.6) | collective-permute-done | bytes 147488 | tf_op jit(solution)/shard_map/ppermute | solution.py:12
  67.9 0.0 copy-done.3
  68.0 0.0 copy-start.2
  68.1 10.7 %fusion.8 = f32[192,3072]{1,0:T(8,128)} fusion(bf16[3072,3072]{1,0:T(8,128)(2,1)} %param.6, bf16[384,3072]{1,0:T(8,128)(2,1)S(1)} %constant_dynamic-update-slice_fusion, s32[]{:T(128)S(6)} %select_n.14), kind=kOutput, calls=%fused_computation.13 | convolution fusion | flops 3623878656 | bytes 22413316 | tf_op jit(solution)/shard_map/dot_general | solution.py:46
  78.7 0.0 copy-done.2
  78.7 0.0 all-gather.2.cloned.1.call-done
  78.7 14.5 %fusion.13 = f32[192,3072]{1,0:T(8,128)} fusion(bf16[192,3072]{1,0:T(8,128)(2,1)} %all-gather.2.cloned.1.call-done, bf16[3072,3072]{1,0:T(8,128)(2,1)} %param.7), kind=kOutput, calls=%fused_computation.34 | convolution fusion | flops 3623878656 | bytes 22413312 | tf_op jit(solution)/shard_map/dot_general | solution.py:30
  93.2 0.0 all-reduce.3.cloned.1.call-update
  93.2 0.0 reduce-scatter.5.cloned.1.call-start
  93.3 114.7 %all-reduce.3.cloned.1.call-done = (f32[192,3072]{1,0:T(8,128)}, f32[192,3072]{1,0:T(8,128)}) async-done(((f32[192,3072]{1,0:T(8,128)}, f32[192,3072]{1,0:T(8,128)}), (f32[192,3072]{1,0:T(8,128)}, f32[192,3072]{1,0:T(8,128)})) %all-reduce.3.cloned.1.call-update) | async-done | bytes 4718608 | tf_op jit(solution)/shard_map/psum | solution.py:48
  208.0 3.9 %fusion.6 = bf16[192,3072]{1,0:T(8,128)(2,1)S(1)} fusion(f32[192,3072]{1,0:T(8,128)} %get-tuple-element.5, f32[192,3072]{1,0:T(8,128)} %get-tuple-element.4), kind=kLoop, calls=%fused_computation.10 | loop fusion | flops 11206656 | bytes 5898240 | tf_op jit(solution)/shard_map/convert_element_type | solution.py:26
  211.9 11.5 %fusion.14 = f32[192,3072]{1,0:T(8,128)} fusion(bf16[192,3072]{1,0:T(8,128)(2,1)S(1)} %fusion.6, bf16[3072,3072]{1,0:T(8,128)(2,1)} %param.6), kind=kOutput, calls=%fused_computation.35 | convolution fusion | flops 3623878656 | bytes 22413312 | tf_op jit(solution)/shard_map/dot_general | solution.py:30
  223.4 0.0 copy-start
  223.4 0.0 reduce-scatter.5.cloned.1.call-update
  223.5 0.2 reduce-scatter.3.cloned.1.call-start
  223.7 1.4 copy-done
  225.1 12.1 %fusion.12 = f32[192,3072]{1,0:T(8,128)} fusion(bf16[3072,3072]{1,0:T(8,128)(2,1)} %param.7, f32[192,3072]{1,0:T(8,128)S(1)} %copy-done), kind=kOutput, calls=%fused_computation.33 | convolution fusion | flops 3629187072 | bytes 23592960 | tf_op jit(solution)/shard_map/dot_general | solution.py:52
  237.2 0.0 reduce-scatter.3.cloned.1.call-update
  237.2 0.0 copy-start.1
  237.2 10.9 %convolution_convert_fusion.1 = bf16[3072,3072]{1,0:T(8,128)(2,1)} fusion(bf16[192,3072]{1,0:T(8,128)(2,1)S(1)} %fusion.6, bf16[384,3072]{1,0:T(8,128)(2,1)} %copy-done.2, s32[]{:T(128)S(6)} %select_n.14), kind=kOutput, calls=%fused_computation.1 | convolution fusion | flops 3633315840 | bytes 21233668 | tf_op jit(solution)/shard_map/dot_general | solution.py:36
  248.2 0.0 copy-done.1
  248.2 9.6 %convolution_convert_fusion = bf16[3072,3072]{1,0:T(8,128)(2,1)} fusion(bf16[192,3072]{1,0:T(8,128)(2,1)S(1)} %copy-done.1, f32[192,3072]{1,0:T(8,128)S(1)} %copy-done), kind=kOutput, calls=%fused_computation | convolution fusion | flops 3638624256 | bytes 22413312 | tf_op jit(solution)/shard_map/dot_general | solution.py:36
  257.7 19.9 %reduce-scatter.5.cloned.1.call-done = f32[24,3072]{1,0:T(8,128)} async-done(((f32[192,3072]{1,0:T(8,128)}), f32[24,3072]{1,0:T(8,128)}) %reduce-scatter.5.cloned.1.call-update) | async-done | bytes 294928 | tf_op jit(solution)/shard_map/reduce_scatter | solution.py:58
  277.6 56.0 %reduce-scatter.3.cloned.1.call-done = f32[24,3072]{1,0:T(8,128)} async-done(((f32[192,3072]{1,0:T(8,128)}), f32[24,3072]{1,0:T(8,128)}) %reduce-scatter.3.cloned.1.call-update) | async-done | bytes 294928 | tf_op jit(solution)/shard_map/reduce_scatter | solution.py:51
  (15 shorter events, 0.2 us)
Async XLA Ops:
  7.2 60.7 %copy-start.3 = (bf16[24,3072]{1,0:T(8,128)(2,1)S(1)}, bf16[24,3072]{1,0:T(8,128)(2,1)}, u32[]{:S(2)}) copy-start(bf16[24,3072]{1,0:T(8,128)(2,1)} %param.4) | copy-start | bytes 442372
  7.2 71.6 %all-gather.2.cloned.1.call-start = ((), (), s32[]{:S(2)}) async-start(), calls=%async_computation.3 | async-start | bytes 1327104 | tf_op jit(solution)/shard_map/all_gather | solution.py:44
  7.9 200.1 %all-reduce.3.cloned.1.call-start = ((), (), s32[]{:S(2)}) async-start(), calls=%async_computation.5 | async-start | bytes 9437184 | tf_op jit(solution)/shard_map/psum | solution.py:48
  8.0 9.1 %collective-permute-start = (bf16[24,3072]{1,0:T(8,128)(2,1)}, bf16[24,3072]{1,0:T(8,128)(2,1)S(1)}, u32[]{:S(2)}, u32[]{:S(2)}) collective-permute-start(bf16[24,3072]{1,0:T(8,128)(2,1)} %param.4), channel_id=1, source_target_pairs={{0,7},{1,0},{2,1},{3,2},{4,3},{5,4},{6,5},{7,6},{8,15},{9,8},{10,9... | collective-permute-start | bytes 442376 | tf_op jit(solution)/shard_map/ppermute | solution.py:12
  17.0 11.1 %collective-permute-start.1 = (bf16[24,3072]{1,0:T(8,128)(2,1)S(1)}, bf16[24,3072]{1,0:T(8,128)(2,1)S(1)}, u32[]{:S(2)}, u32[]{:S(2)}) collective-permute-start(bf16[24,3072]{1,0:T(8,128)(2,1)S(1)} %collective-permute-done), channel_id=1, source_target_pairs={{0,7},{1,0},{2,1},{3,2},{4,3},{5,4},{6,5},{7,6},{8,15},{9,8},{10,9... | collective-permute-start | bytes 442376 | tf_op jit(solution)/shard_map/ppermute | solution.py:12
  28.1 9.8 %collective-permute-start.2 = (bf16[24,3072]{1,0:T(8,128)(2,1)S(1)}, bf16[24,3072]{1,0:T(8,128)(2,1)S(1)}, u32[]{:S(2)}, u32[]{:S(2)}) collective-permute-start(bf16[24,3072]{1,0:T(8,128)(2,1)S(1)} %collective-permute-done.1), channel_id=1, source_target_pairs={{0,7},{1,0},{2,1},{3,2},{4,3},{5,4},{6,5},{7,6},{8,15},{9,8},{10,9... | collective-permute-start | bytes 442376 | tf_op jit(solution)/shard_map/ppermute | solution.py:12
  37.9 7.0 %collective-permute-start.3 = (bf16[24,3072]{1,0:T(8,128)(2,1)S(1)}, bf16[24,3072]{1,0:T(8,128)(2,1)S(1)}, u32[]{:S(2)}, u32[]{:S(2)}) collective-permute-start(bf16[24,3072]{1,0:T(8,128)(2,1)S(1)} %collective-permute-done.2), channel_id=1, source_target_pairs={{0,7},{1,0},{2,1},{3,2},{4,3},{5,4},{6,5},{7,6},{8,15},{9,8},{10,9... | collective-permute-start | bytes 442376 | tf_op jit(solution)/shard_map/ppermute | solution.py:12
  44.9 7.7 %collective-permute-start.4 = (bf16[24,3072]{1,0:T(8,128)(2,1)S(1)}, bf16[24,3072]{1,0:T(8,128)(2,1)S(1)}, u32[]{:S(2)}, u32[]{:S(2)}) collective-permute-start(bf16[24,3072]{1,0:T(8,128)(2,1)S(1)} %collective-permute-done.3), channel_id=1, source_target_pairs={{0,7},{1,0},{2,1},{3,2},{4,3},{5,4},{6,5},{7,6},{8,15},{9,8},{10,9... | collective-permute-start | bytes 442376 | tf_op jit(solution)/shard_map/ppermute | solution.py:12
  52.6 7.7 %collective-permute-start.5 = (bf16[24,3072]{1,0:T(8,128)(2,1)S(1)}, bf16[24,3072]{1,0:T(8,128)(2,1)S(1)}, u32[]{:S(2)}, u32[]{:S(2)}) collective-permute-start(bf16[24,3072]{1,0:T(8,128)(2,1)S(1)} %collective-permute-done.4), channel_id=1, source_target_pairs={{0,7},{1,0},{2,1},{3,2},{4,3},{5,4},{6,5},{7,6},{8,15},{9,8},{10,9... | collective-permute-start | bytes 442376 | tf_op jit(solution)/shard_map/ppermute | solution.py:12
  60.2 7.7 %collective-permute-start.6 = (bf16[24,3072]{1,0:T(8,128)(2,1)S(1)}, bf16[24,3072]{1,0:T(8,128)(2,1)S(1)}, u32[]{:S(2)}, u32[]{:S(2)}) collective-permute-start(bf16[24,3072]{1,0:T(8,128)(2,1)S(1)} %collective-permute-done.5), channel_id=1, source_target_pairs={{0,7},{1,0},{2,1},{3,2},{4,3},{5,4},{6,5},{7,6},{8,15},{9,8},{10,9... | collective-permute-start | bytes 442376 | tf_op jit(solution)/shard_map/ppermute | solution.py:12
  68.0 10.7 %copy-start.2 = (bf16[384,3072]{1,0:T(8,128)(2,1)}, bf16[384,3072]{1,0:T(8,128)(2,1)S(1)}, u32[]{:S(2)}) copy-start(bf16[384,3072]{1,0:T(8,128)(2,1)S(1)} %constant_dynamic-update-slice_fusion) | copy-start | bytes 7077892
  93.2 184.4 %reduce-scatter.5.cloned.1.call-start = ((), (), s32[]{:S(2)}) async-start(), calls=%async_computation.4 | async-start | bytes 2654208 | tf_op jit(solution)/shard_map/reduce_scatter | solution.py:58
  223.4 1.7 copy-start
  223.5 110.1 %reduce-scatter.3.cloned.1.call-start = ((), (), s32[]{:S(2)}) async-start(), calls=%async_computation.2 | async-start | bytes 2654208 | tf_op jit(solution)/shard_map/reduce_scatter | solution.py:51
  237.2 10.9 %copy-start.1 = (bf16[192,3072]{1,0:T(8,128)(2,1)S(1)}, bf16[192,3072]{1,0:T(8,128)(2,1)}, u32[]{:S(2)}) copy-start(bf16[192,3072]{1,0:T(8,128)(2,1)} %all-gather.2.cloned.1.call-done) | copy-start | bytes 3538948
Sparse Core Ops, SparseCore 0:
  9.6 28.5 all-gather.1
  93.4 114.6 all-reduce.2
  223.6 54.0 reduce-scatter.4
  280.4 53.1 reduce-scatter.2
